TPU v7x, 32 devices: a whole 2x2x4 slice. The times are simulated.
32 devices in a mesh: row: 4 (over y, x), col: 8 (over z, core).
Axes of the slice: x: 2, y: 2, z: 4, core: 2. Of those that a mesh axis runs over, the one named last changes fastest.
Arguments:
- increment: float32 [4, 60, 32, 1024], P(None, None, 'row', 'col'), may hold values from -6 to 6
- residual: float32 [4, 60, 32, 1024], P(None, None, 'row', 'col'), may hold values from -6 to 6
- direction: float32 [4, 60, 32, 1024], P(None, None, 'row', 'col'), may hold values from -6 to 6
- lanczos: bfloat16 [10, 4, 60, 32, 1024], P(None, None, None, 'row', 'col'), may hold values from -10 to 10
- vertical_modes: float32 [4, 60, 60], replicated, may hold values from -0.75 to 0.75
- amplitude: float32 [4, 60], replicated, may hold values from 0.5 to 2
- length_east: float32 [4, 8], replicated, may hold values from 0.25 to 4
- length_north: float32 [4, 8], replicated, may hold values from 0.25 to 4
- observed_cell: int32 [16384], P(('row', 'col')), may hold values from 0 to 245759
- observed_weight: float32 [16384], P(('row', 'col')), may hold values from 0.5 to 4
- observed_count: int32 [32], P(('row', 'col')), may hold values from 128 to 512, as said below
Outputs:
- new_increment: float32 [4, 60, 32, 1024], P(None, None, 'row', 'col')
- new_residual: float32 [4, 60, 32, 1024], P(None, None, 'row', 'col')
- new_direction: float32 [4, 60, 32, 1024], P(None, None, 'row', 'col')
Inputs may be any that keep to these rules, and one draw needn't show every extreme that they name: observed_cell[s] indexes a cell of the tile that slot s belongs to. `observed_count`: a tile has at most 512 live slots, and some tile has exactly 512.
All inputs are finite; a program needn't handle non-finite values.
Results may differ from a plain program's by a relative error of at most 0.00055.
Values sent between devices are 32-bit elements; how exact they have to be, the bound alone decides.
A program may use at most 128 MiB of HBM per device.

v0:
```python
import functools

import jax
import jax.numpy as jnp
from jax import lax
from jax.experimental import pallas as pl
from jax.experimental.pallas import tpu as pltpu
from jax.sharding import PartitionSpec as P

MESH = pl.DeviceIdType.MESH
f32 = jnp.float32
bf16 = jnp.bfloat16
CHUNK = 32


def kernel(
    R, C, V, L, M, K, ny, nx, total_cells,
    dir_ref, tab_ref, vm_ref, amp_ref, cell_ref, wgt_ref, cnt_ref,
    res_hbm, inc_hbm, lz_hbm,
    oinc_hbm, ores_hbm, odir_hbm,
    res_ref, inc_ref, lz_ref, oinc_ref, ores_ref, odir_ref,
    img_ref, lead_ref, mom_ref, hot_ref, wsum_ref,
    es_ref, er_ref, ns_ref, nr_ref, rs_ref, rr_ref,
    load_sem, out_sem, e_ssem, e_rsem, n_ssem, n_rsem, r_ssem, r_rsem,
):
    N = R * C
    I = V * M
    row, col = lax.axis_index("row"), lax.axis_index("col")
    me = row * C + col
    barrier = pltpu.get_barrier_semaphore()

    def place(d):
        peer = lax.rem(me + d, N)
        return (lax.div(peer, C), lax.rem(peer, C))

    def greet(d, carry):
        pl.semaphore_signal(barrier, inc=1, device_id=place(d), device_id_type=MESH)
        return carry

    lax.fori_loop(1, N, greet, 0)
    loads = [
        pltpu.make_async_copy(res_hbm, res_ref, load_sem.at[0]),
        pltpu.make_async_copy(lz_hbm, lz_ref, load_sem.at[1]),
        pltpu.make_async_copy(inc_hbm, inc_ref, load_sem.at[2]),
    ]
    for load in loads:
        load.start()

    lane = lax.broadcasted_iota(jnp.int32, (1, 1, nx), 2)
    sub = lax.broadcasted_iota(jnp.int32, (1, ny, 1), 1)

    def log_alpha(which):
        return tab_ref[which].reshape(I, ny, nx)

    def scans(u, which):
        axis, size, at = ((2, nx, lane), (1, ny, sub))[which]
        power = jnp.exp(log_alpha(which))
        f, g = u, u
        shift = 1
        while shift < size:
            f = f + power * jnp.where(at >= shift, pltpu.roll(f, shift, axis), 0.0)
            g = g + power * jnp.where(at < size - shift, pltpu.roll(g, size - shift, axis), 0.0)
            power = power * power
            shift *= 2
        return f, g

    def combine(first, second, log_small, index, count, size, own, received):
        at = index.astype(f32)
        left = jnp.zeros_like(log_small)
        right = jnp.zeros_like(log_small)
        edge = jnp.zeros_like(log_small)
        for d in range(count):
            e, b, e_edge = own if d == 0 else received(d)
            wraps = d > index
            source = jnp.where(wraps, index - d + count, index - d).astype(f32)
            if d > 0:
                left += jnp.where(wraps, 0.0, jnp.exp(log_small * float(size * (d - 1)))) * e
                right += jnp.where(wraps, jnp.exp(log_small * float(size * (count - d - 1))), 0.0) * b
            edge += jnp.exp(log_small * (float(size * (count - 1)) - size * source + 1.0)) * e_edge
        right -= jnp.exp(log_small * (size * (float(count - 1) - at))) * edge
        return left, right

    def line_scale(which):
        a = jnp.exp(log_alpha(which))
        return jnp.sqrt((1.0 - a) / (1.0 + a))

    def east_copies(inst):
        return [
            pltpu.make_async_remote_copy(
                src_ref=es_ref.at[inst],
                dst_ref=er_ref.at[inst, d],
                send_sem=e_ssem.at[inst, d],
                recv_sem=e_rsem.at[inst, d],
                device_id=(row, lax.rem(col + d, C)),
                device_id_type=MESH,
            )
            for d in range(1, C)
        ]

    def north_copies(inst):
        return [
            pltpu.make_async_remote_copy(
                src_ref=ns_ref.at[inst],
                dst_ref=nr_ref.at[inst, d],
                send_sem=n_ssem.at[inst, d],
                recv_sem=n_rsem.at[inst, d],
                device_id=(lax.rem(row + d, R), col),
                device_id_type=MESH,
            )
            for d in range(1, R)
        ]

    small_lane = lax.broadcasted_iota(jnp.int32, (ny, nx), 1)

    def east_start(u, inst):
        f, g = scans(u, 0)
        first = jnp.zeros((ny, nx), f32)
        second = jnp.zeros((ny, nx), f32)
        for i in range(I):
            e = jnp.broadcast_to(f[i, :, nx - 1 : nx], (ny, nx))
            b = jnp.broadcast_to(g[i, :, 0:1], (ny, nx))
            first = jnp.where(small_lane == i, e, first)
            first = jnp.where(small_lane == I + i, b, first)
            second = jnp.where(small_lane == I + i, e, second)
        es_ref[inst, 0] = first
        es_ref[inst, 1] = second
        lead_ref[...] = (f + g - u).reshape(I * ny, nx)
        return east_copies(inst)

    def east_finish(inst, copies):
        for copy in copies:
            copy.wait()
        log_small = jnp.zeros((ny, nx), f32)
        for i in range(I):
            hit = (small_lane == i) | (small_lane == I + i)
            log_small = jnp.where(hit, tab_ref[0, i * ny : (i + 1) * ny, :], log_small)
        left, right = combine(
            None, None, log_small, col, C, nx,
            (es_ref[inst, 0], es_ref[inst, 0], es_ref[inst, 1]),
            lambda d: (er_ref[inst, d, 0], er_ref[inst, d, 0], er_ref[inst, d, 1]),
        )
        at = lax.broadcasted_iota(jnp.int32, (ny, nx), 1).astype(f32)
        for i in range(I):
            rows = slice(i * ny, (i + 1) * ny)
            log_a = tab_ref[0, rows, :]
            x = jnp.broadcast_to(left[:, i : i + 1], (ny, nx))
            y = jnp.broadcast_to(right[:, I + i : I + i + 1], (ny, nx))
            a = jnp.exp(log_a)
            lead_ref[rows, :] = jnp.sqrt((1.0 - a) / (1.0 + a)) * (
                lead_ref[rows, :]
                + jnp.exp(log_a * (at + 1.0)) * x
                + jnp.exp(log_a * (float(nx) - at)) * y
            )

    def north_start(u, inst):
        f, g = scans(u, 1)
        mom_ref[0] = f.reshape(I * ny, nx)
        mom_ref[1] = g.reshape(I * ny, nx)
        ns_ref[inst, 0] = mom_ref[0, pl.ds(ny - 1, I, stride=ny), :]
        ns_ref[inst, 1] = mom_ref[1, pl.ds(0, I, stride=ny), :]
        lead_ref[...] = (f + g - u).reshape(I * ny, nx)
        return north_copies(inst)

    def north_finish(inst, copies):
        for copy in copies:
            copy.wait()
        log_small = tab_ref[1, pl.ds(0, I, stride=ny), :]
        left, right = combine(
            None, None, log_small, row, R, ny,
            (ns_ref[inst, 0], ns_ref[inst, 1], ns_ref[inst, 0]),
            lambda d: (nr_ref[inst, d, 0], nr_ref[inst, d, 1], nr_ref[inst, d, 0]),
        )
        at = lax.broadcasted_iota(jnp.int32, (ny, nx), 0).astype(f32)
        for i in range(I):
            rows = slice(i * ny, (i + 1) * ny)
            log_a = tab_ref[1, rows, :]
            x = jnp.broadcast_to(left[i : i + 1, :], (ny, nx))
            y = jnp.broadcast_to(right[i : i + 1, :], (ny, nx))
            a = jnp.exp(log_a)
            lead_ref[rows, :] = jnp.sqrt((1.0 - a) / (1.0 + a)) * (
                lead_ref[rows, :]
                + jnp.exp(log_a * (at + 1.0)) * x
                + jnp.exp(log_a * (float(ny) - at)) * y
            )

    plane = L * ny
    u = jnp.concatenate([dir_ref[v * plane : v * plane + M * ny, :] for v in range(V)], axis=0)
    copies = east_start(u.reshape(I, ny, nx), 0)
    pl.semaphore_wait(barrier, N - 1)
    for copy in copies:
        copy.start()

    cell = cell_ref[...]
    slots = cell.shape[1]
    level = lax.shift_right_logical(cell, (ny * nx).bit_length() - 1)
    spot = cell & (ny * nx - 1)
    hot_ref[...] = jnp.where(
        lax.broadcasted_iota(jnp.int32, (ny * nx, slots), 0) == spot, 1.0, 0.0
    ).astype(bf16)
    live = lax.broadcasted_iota(jnp.int32, (1, slots), 1) < cnt_ref[0]
    weight = jnp.where(live, wgt_ref[...], 0.0)
    parts = []
    rest = weight
    for _ in range(3):
        part = rest.astype(bf16).astype(f32)
        parts.append(part)
        rest = rest - part
    nt = (((1,), (1,)), ((), ()))
    for v in range(V):
        hit = lax.broadcasted_iota(jnp.int32, (L, slots), 0) + v * L == level
        wsum_ref[v] = sum(
            lax.dot_general(
                jnp.where(hit, part, 0.0).astype(bf16), hot_ref[...], nt,
                preferred_element_type=f32,
            )
            for part in parts
        )

    east_finish(0, copies)
    copies = north_start(lead_ref[...].reshape(I, ny, nx), 0)
    for copy in copies:
        copy.start()
    north_finish(0, copies)

    for v in range(V):
        mixed = vm_ref[v] * amp_ref[v : v + 1, :]
        field = jnp.concatenate(
            [
                jnp.concatenate(
                    [
                        lead_ref[pl.ds(v * M * ny + y, M, stride=ny), :],
                        dir_ref[pl.ds(v * plane + M * ny + y, L - M, stride=ny), :],
                    ],
                    axis=0,
                )
                for y in range(ny)
            ],
            axis=1,
        )
        grid = lax.dot_general(
            mixed, field, (((1,), (0,)), ((), ())),
            precision=lax.Precision.HIGHEST, preferred_element_type=f32,
        )
        spread = grid * wsum_ref[v]
        back = lax.dot_general(
            mixed.T, spread, (((1,), (0,)), ((), ())),
            precision=lax.Precision.HIGHEST, preferred_element_type=f32,
        )
        for y in range(ny):
            img_ref[pl.ds(v * plane + y, L, stride=ny), :] = back[:, y * nx : (y + 1) * nx]

    u = jnp.concatenate([img_ref[v * plane : v * plane + M * ny, :] for v in range(V)], axis=0)
    copies = north_start(u.reshape(I, ny, nx), 1)
    for copy in copies:
        copy.start()

    steps = V * plane // CHUNK

    def fold(x):
        return jnp.sum(x.reshape(CHUNK // 8, 8, nx), axis=0)

    loads[0].wait()
    loads[1].wait()
    zero = jnp.zeros((8, nx), f32)

    def first_dots(s, carry):
        rows = pl.ds(pl.multiple_of(s * CHUNK, CHUNK), CHUNK)
        r = res_ref[rows, :]
        out = [carry[0] + fold(r * r)]
        for k in range(K):
            out.append(carry[k + 1] + fold(r * lz_ref[k, rows, :].astype(f32)))
        return tuple(out)

    res_dots = lax.fori_loop(0, steps, first_dots, (zero,) * (K + 1))

    north_finish(1, copies)
    copies = east_start(lead_ref[...].reshape(I, ny, nx), 1)
    for copy in copies:
        copy.start()
    east_finish(1, copies)
    for v in range(V):
        img_ref[v * plane : v * plane + M * ny, :] = lead_ref[v * M * ny : (v + 1) * M * ny, :]

    def second_dots(s, carry):
        rows = pl.ds(pl.multiple_of(s * CHUNK, CHUNK), CHUNK)
        d = dir_ref[rows, :]
        image = d + img_ref[rows, :]
        img_ref[rows, :] = image
        out = [carry[0] + fold(d * image)]
        for k in range(K):
            out.append(carry[k + 1] + fold(image * lz_ref[k, rows, :].astype(f32)))
        return tuple(out)

    img_dots = lax.fori_loop(0, steps, second_dots, (zero,) * (K + 1))

    def reduce_copy(inst, d):
        return pltpu.make_async_remote_copy(
            src_ref=rs_ref.at[inst],
            dst_ref=rr_ref.at[inst, d],
            send_sem=r_ssem.at[inst, d],
            recv_sem=r_rsem.at[inst, d],
            device_id=place(d),
            device_id_type=MESH,
        )

    def reduce_start(inst):
        def go(d, carry):
            reduce_copy(inst, d).start()
            return carry

        lax.fori_loop(1, N, go, 0)

    def reduce_finish(inst):
        def go(d, carry):
            reduce_copy(inst, d).wait()
            return carry

        lax.fori_loop(1, N, go, 0)
        rr_ref[inst, 0] = rs_ref[inst]
        return jnp.sum(rr_ref[inst], axis=0)

    sums = list(res_dots) + list(img_dots)
    small_sub = lax.broadcasted_iota(jnp.int32, (8, nx), 0)
    packed = zero
    for n, part in enumerate(sums):
        here = (small_sub == n % 8) & (small_lane == n // 8)
        packed = jnp.where(here, jnp.sum(part, axis=(0, 1), keepdims=True), packed)
    rs_ref[0] = packed
    reduce_start(0)
    loads[2].wait()
    totals = reduce_finish(0)

    def total(n):
        return totals[n % 8 : n % 8 + 1, n // 8 : n // 8 + 1]

    norm_old = total(0)
    step_size = norm_old / total(K + 1)
    coefficient = [
        jnp.broadcast_to((total(k + 1) - step_size * total(K + 2 + k)) / total_cells, (CHUNK, nx))
        for k in range(K)
    ]
    step_wide = jnp.broadcast_to(step_size, (CHUNK, nx))

    def update(s, carry):
        rows = pl.ds(pl.multiple_of(s * CHUNK, CHUNK), CHUNK)
        oinc_ref[rows, :] = inc_ref[rows, :] + step_wide * dir_ref[rows, :]
        moved = res_ref[rows, :] - step_wide * img_ref[rows, :]
        for k in range(K):
            moved = moved - coefficient[k] * lz_ref[k, rows, :].astype(f32)
        ores_ref[rows, :] = moved
        return carry + fold(moved * moved)

    norm_part = lax.fori_loop(0, steps, update, zero)
    rs_ref[1] = jnp.broadcast_to(jnp.sum(norm_part, axis=(0, 1), keepdims=True), (8, nx))
    reduce_start(1)
    stores = [
        pltpu.make_async_copy(oinc_ref, oinc_hbm, out_sem.at[0]),
        pltpu.make_async_copy(ores_ref, ores_hbm, out_sem.at[1]),
        pltpu.make_async_copy(odir_ref, odir_hbm, out_sem.at[2]),
    ]
    stores[0].start()
    stores[1].start()
    ratio = jnp.broadcast_to(reduce_finish(1)[0:1, 0:1] / norm_old, (CHUNK, nx))

    def turn(s, carry):
        rows = pl.ds(pl.multiple_of(s * CHUNK, CHUNK), CHUNK)
        odir_ref[rows, :] = ores_ref[rows, :] + ratio * dir_ref[rows, :]
        return carry

    lax.fori_loop(0, steps, turn, 0)
    stores[2].start()
    for store in stores:
        store.wait()


def local(
    R, C,
    increment, residual, direction, lanczos, vertical_modes, amplitude,
    length_east, length_north, observed_cell, observed_weight, observed_count,
):
    V, L, ny, nx = direction.shape
    M = length_east.shape[1]
    K = lanczos.shape[0]
    I = V * M
    N = R * C
    flat = V * L * ny
    slots = observed_cell.shape[0]
    logs = jnp.stack([-1.0 / (length_east * nx), -1.0 / (length_north * ny)])
    table = jnp.broadcast_to(logs.reshape(2, I, 1, 1), (2, I, ny, nx)).reshape(2, I * ny, nx)
    vmem = pl.BlockSpec(memory_space=pltpu.VMEM)
    hbm = pl.BlockSpec(memory_space=pl.ANY)
    smem = pl.BlockSpec(memory_space=pltpu.SMEM)
    field = jax.ShapeDtypeStruct((flat, nx), f32)
    big = pltpu.VMEM((flat, nx), f32)
    out = pl.pallas_call(
        functools.partial(kernel, R, C, V, L, M, K, ny, nx, float(flat * nx * N)),
        out_shape=(field,) * 3,
        in_specs=[vmem] * 6 + [smem] + [hbm] * 3,
        out_specs=(hbm,) * 3,
        scratch_shapes=[
            big, big, pltpu.VMEM((K, flat, nx), bf16), big, big, big,
            big, pltpu.VMEM((I * ny, nx), f32), pltpu.VMEM((2, I * ny, nx), f32),
            pltpu.VMEM((ny * nx, slots), bf16), pltpu.VMEM((V, L, ny * nx), f32),
            pltpu.VMEM((2, 2, ny, nx), f32), pltpu.VMEM((2, C, 2, ny, nx), f32),
            pltpu.VMEM((2, 2, I, nx), f32), pltpu.VMEM((2, R, 2, I, nx), f32),
            pltpu.VMEM((2, 8, nx), f32), pltpu.VMEM((2, N, 8, nx), f32),
            pltpu.SemaphoreType.DMA((3,)), pltpu.SemaphoreType.DMA((3,)),
            pltpu.SemaphoreType.DMA((2, C)), pltpu.SemaphoreType.DMA((2, C)),
            pltpu.SemaphoreType.DMA((2, R)), pltpu.SemaphoreType.DMA((2, R)),
            pltpu.SemaphoreType.DMA((2, N)), pltpu.SemaphoreType.DMA((2, N)),
        ],
        compiler_params=pltpu.CompilerParams(
            collective_id=0, has_side_effects=True, vmem_limit_bytes=48 * 2**20
        ),
    )(
        direction.reshape(flat, nx), table, vertical_modes, amplitude,
        observed_cell.reshape(1, slots), observed_weight.reshape(1, slots), observed_count,
        residual.reshape(flat, nx), increment.reshape(flat, nx), lanczos.reshape(K, flat, nx),
    )
    return tuple(x.reshape(direction.shape) for x in out)


def solution(mesh):
    field = P(None, None, "row", "col")
    tile = P(("row", "col"))
    in_specs = (
        field, field, field, P(None, None, None, "row", "col"),
        P(), P(), P(), P(), tile, tile, tile,
    )
    return jax.shard_map(
        functools.partial(local, mesh.shape["row"], mesh.shape["col"]),
        mesh=mesh, in_specs=in_specs, out_specs=(field,) * 3, check_vma=False,
    )
```

profile of v0, /device:TPU:0, one launch (start us, length us, event | category | flops | bytes accessed | tf_op | source)
XLA Modules:
  0.0 53.6 jit_solution(16564429791077602941)
XLA Ops:
  1.3 0.7 %multiply_divide_fusion.1 = f32[4,8]{1,0:T(4,128)S(1)} fusion(f32[4,8]{1,0:T(4,128)} %param.17), kind=kLoop, calls=%fused_computation.1 | loop fusion | flops 64 | bytes 256 | tf_op jit(solution)/shard_map/div | solution.py:388
  2.0 0.1 stack.9
  2.0 0.7 %multiply_divide_fusion = f32[4,8]{1,0:T(4,128)S(1)} fusion(f32[4,8]{1,0:T(4,128)} %param.18), kind=kLoop, calls=%fused_computation | loop fusion | flops 64 | bytes 256 | tf_op jit(solution)/shard_map/div | solution.py:388
  2.7 0.1 stack.10
  2.8 0.1 broadcast_in_dim.12
  2.9 0.1 broadcast_in_dim.13
  3.0 0.9 %copy.15.vm_ref = f32[4,60,60]{2,1,0:T(8,128)S(1)} copy(f32[4,60,60]{2,0,1:T(4,128)} %param.15) | data formatting | bytes 115200 | tf_op args[4]
  3.9 0.1 broadcast_in_dim.14.tab_ref
  4.1 0.0 copy-start
  4.1 1.2 %copy-done = f32[4,60,8,128]{3,2,1,0:T(8,128)S(1)} copy-done((f32[4,60,8,128]{3,2,1,0:T(8,128)S(1)}, f32[4,60,8,128]{3,2,1,0:T(8,128)}, u32[]{:S(2)}) %copy-start) | copy-done | bytes 983064
  5.3 0.0 copy-start.1
  5.3 1.2 %copy-done.1 = f32[4,60,8,128]{3,2,1,0:T(8,128)S(1)} copy-done((f32[4,60,8,128]{3,2,1,0:T(8,128)S(1)}, f32[4,60,8,128]{3,2,1,0:T(8,128)}, u32[]{:S(2)}) %copy-start.1) | copy-done | bytes 983064
  6.5 0.0 copy-start.2
  6.5 0.7 %copy-done.2 = f32[4,60]{1,0:T(4,128)S(1)} copy-done((f32[4,60]{1,0:T(4,128)S(1)}, f32[4,60]{1,0:T(4,128)}, u32[]{:S(2)}) %copy-start.2) | copy-done | bytes 984
  7.2 0.0 copy-start.3
  7.2 0.7 %copy-done.3 = s32[512]{0:T(512)S(1)} copy-done((s32[512]{0:T(512)S(1)}, s32[512]{0:T(512)}, u32[]{:S(2)}) %copy-start.3) | copy-done | bytes 2072
  7.8 0.0 copy-start.4
  7.8 0.7 %copy-done.4 = f32[512]{0:T(512)S(1)} copy-done((f32[512]{0:T(512)S(1)}, f32[512]{0:T(512)}, u32[]{:S(2)}) %copy-start.4) | copy-done | bytes 2072
  8.5 42.2 %shard_map.130 = (f32[1920,128]{1,0:T(8,128)S(1)}, f32[1920,128]{1,0:T(8,128)S(1)}, f32[1920,128]{1,0:T(8,128)S(1)}) custom-call(f32[1920,128]{1,0:T(8,128)S(1)} %bitcast.10, f32[2,256,128]{2,1,0:T(8,128)S(1)} %broadcast_in_dim.14.tab_ref, f32[4,60,60]{2,1,0:T(8,128)S(1)} %copy.15.vm_ref, f32[4,60]{1,0:T(4,128)S(1)} %copy-done.2, s32[1,512]{1,0:T(1,128)S(1)} %bitcast.15, ...), custom_call_target="tpu_custom_call" | custom-call | tf_op jit(solution)/shard_map/pallas_call | solution.py:395
  50.7 0.9 %copy.20 = f32[4,60,8,128]{3,2,1,0:T(8,128)} copy(f32[4,60,8,128]{3,2,1,0:T(8,128)S(1)} %bitcast.14) | data formatting | bytes 1966080
  51.7 0.9 %copy.21 = f32[4,60,8,128]{3,2,1,0:T(8,128)} copy(f32[4,60,8,128]{3,2,1,0:T(8,128)S(1)} %bitcast.13) | data formatting | bytes 1966080
  52.6 0.9 %copy.22 = f32[4,60,8,128]{3,2,1,0:T(8,128)} copy(f32[4,60,8,128]{3,2,1,0:T(8,128)S(1)} %bitcast.12) | data formatting | bytes 1966080
  (1 shorter events, 0.0 us)
Async XLA Ops:
  4.1 1.2 %copy-start = (f32[4,60,8,128]{3,2,1,0:T(8,128)S(1)}, f32[4,60,8,128]{3,2,1,0:T(8,128)}, u32[]{:S(2)}) copy-start(f32[4,60,8,128]{3,2,1,0:T(8,128)} %param.13) | copy-start | bytes 2949124
  5.3 1.2 %copy-start.1 = (f32[4,60,8,128]{3,2,1,0:T(8,128)S(1)}, f32[4,60,8,128]{3,2,1,0:T(8,128)}, u32[]{:S(2)}) copy-start(f32[4,60,8,128]{3,2,1,0:T(8,128)} %param.12) | copy-start | bytes 2949124
  6.5 0.7 %copy-start.2 = (f32[4,60]{1,0:T(4,128)S(1)}, f32[4,60]{1,0:T(4,128)}, u32[]{:S(2)}) copy-start(f32[4,60]{1,0:T(4,128)} %amp_ref.1) | copy-start | bytes 2884
  7.2 0.7 %copy-start.3 = (s32[512]{0:T(512)S(1)}, s32[512]{0:T(512)}, u32[]{:S(2)}) copy-start(s32[512]{0:T(512)} %param.19) | copy-start | bytes 6148
  7.8 0.7 %copy-start.4 = (f32[512]{0:T(512)S(1)}, f32[512]{0:T(512)}, u32[]{:S(2)}) copy-start(f32[512]{0:T(512)} %param.20) | copy-start | bytes 6148
where the time goes:
time: 53.9 us; the launch traced here: 53.6 us
  Pallas kernels  42.2 us (78%)
  local copies, waits for them, and re-layouts  8.66 us (16%)
  other arithmetic  1.39 us (3%)
  between operations  1.32 us (2%)
    pallas_call x1, Pallas kernels, local(): pl.pallas_call(functools.partial(kernel, R, C, V, L, M, K, ny, nx, float(...  42.2 us
    unnamed x14, local copies, waits for them, and re-layouts  8.19 us
    div x2, other arithmetic, local(): logs = jnp.stack([-1.0 / (length_east * nx), -1.0 / (length_north * ny)])  1.38 us

commit v1 on v0

--- a/solution.py
+++ b/solution.py
@@ -15,16 +15,21 @@
 
 def kernel(
     R, C, V, L, M, K, ny, nx, total_cells,
-    dir_ref, tab_ref, vm_ref, amp_ref, cell_ref, wgt_ref, cnt_ref,
+    cnt_ref, dir_hbm, len_e_hbm, len_n_hbm, vm_hbm, amp_hbm, cell_hbm, wgt_hbm,
     res_hbm, inc_hbm, lz_hbm,
-    oinc_hbm, ores_hbm, odir_hbm,
-    res_ref, inc_ref, lz_ref, oinc_ref, ores_ref, odir_ref,
+    oinc_all, ores_all, odir_all,
+    dir_ref, len_ref, vm_ref, amp_ref, cell_ref, wgt_ref,
+    tab_ref, own_ref, near_ref, far_ref, mix_ref,
+    res_ref, inc_ref, lz_ref,
     img_ref, lead_ref, mom_ref, hot_ref, wsum_ref,
     es_ref, er_ref, ns_ref, nr_ref, rs_ref, rr_ref,
-    load_sem, out_sem, e_ssem, e_rsem, n_ssem, n_rsem, r_ssem, r_rsem,
+    load_sem, e_ssem, e_rsem, n_ssem, n_rsem, r_ssem, r_rsem,
 ):
     N = R * C
     I = V * M
+    oinc_ref, ores_ref, odir_ref = (
+        x.reshape(V * L * ny, nx) for x in (oinc_all, ores_all, odir_all)
+    )
     row, col = lax.axis_index("row"), lax.axis_index("col")
     me = row * C + col
     barrier = pltpu.get_barrier_semaphore()
@@ -37,14 +42,43 @@
         pl.semaphore_signal(barrier, inc=1, device_id=place(d), device_id_type=MESH)
         return carry
 
-    lax.fori_loop(1, N, greet, 0)
+    plane = L * ny
+    lead_rows = M * ny
+    firsts = [
+        pltpu.make_async_copy(len_e_hbm, len_ref.at[0], load_sem.at[3]),
+        pltpu.make_async_copy(len_n_hbm, len_ref.at[1], load_sem.at[4]),
+    ]
+    others = [
+        pltpu.make_async_copy(cell_hbm, cell_ref, load_sem.at[5]),
+        pltpu.make_async_copy(wgt_hbm, wgt_ref, load_sem.at[6]),
+        pltpu.make_async_copy(vm_hbm, vm_ref, load_sem.at[7]),
+        pltpu.make_async_copy(amp_hbm, amp_ref, load_sem.at[8]),
+    ]
+    for v in range(V):
+        part = pl.ds(v * plane, lead_rows)
+        firsts.append(
+            pltpu.make_async_copy(dir_hbm.at[part], dir_ref.at[part], load_sem.at[9 + v])
+        )
+        part = pl.ds(v * plane + lead_rows, plane - lead_rows)
+        others.append(
+            pltpu.make_async_copy(dir_hbm.at[part], dir_ref.at[part], load_sem.at[9 + V + v])
+        )
     loads = [
         pltpu.make_async_copy(res_hbm, res_ref, load_sem.at[0]),
         pltpu.make_async_copy(lz_hbm, lz_ref, load_sem.at[1]),
         pltpu.make_async_copy(inc_hbm, inc_ref, load_sem.at[2]),
     ]
-    for load in loads:
+    for load in firsts + others + loads:
         load.start()
+    lax.fori_loop(1, N, greet, 0)
+    for load in firsts:
+        load.wait()
+    for i in range(I):
+        v, m = i // M, i % M
+        rows = slice(i * ny, (i + 1) * ny)
+        for which, size in ((0, nx), (1, ny)):
+            length = jnp.broadcast_to(len_ref[which, v : v + 1, m : m + 1], (ny, nx))
+            tab_ref[which, rows, :] = -1.0 / (length * float(size))
 
     lane = lax.broadcasted_iota(jnp.int32, (1, 1, nx), 2)
     sub = lax.broadcasted_iota(jnp.int32, (1, ny, 1), 1)
@@ -64,25 +98,46 @@
             shift *= 2
         return f, g
 
-    def combine(first, second, log_small, index, count, size, own, received):
+    def weights(log_small, index, count, size):
         at = index.astype(f32)
-        left = jnp.zeros_like(log_small)
-        right = jnp.zeros_like(log_small)
-        edge = jnp.zeros_like(log_small)
+        left, right, edge = [None], [None], []
+        back = jnp.exp(log_small * (size * (float(count - 1) - at)))
         for d in range(count):
-            e, b, e_edge = own if d == 0 else received(d)
             wraps = d > index
             source = jnp.where(wraps, index - d + count, index - d).astype(f32)
             if d > 0:
-                left += jnp.where(wraps, 0.0, jnp.exp(log_small * float(size * (d - 1)))) * e
-                right += jnp.where(wraps, jnp.exp(log_small * float(size * (count - d - 1))), 0.0) * b
-            edge += jnp.exp(log_small * (float(size * (count - 1)) - size * source + 1.0)) * e_edge
-        right -= jnp.exp(log_small * (size * (float(count - 1) - at))) * edge
+                left.append(jnp.where(wraps, 0.0, jnp.exp(log_small * float(size * (d - 1)))))
+                right.append(
+                    jnp.where(wraps, jnp.exp(log_small * float(size * (count - d - 1))), 0.0)
+                )
+            edge.append(
+                back * jnp.exp(log_small * (float(size * (count - 1)) - size * source + 1.0))
+            )
+        return left, right, edge
+
+    def combine(table, own, received, copies):
+        left_w, right_w, edge_w = table
+        e, b, e_edge = own
+        left = jnp.zeros_like(e)
+        right = -edge_w[0] * e_edge
+        for d, copy in enumerate(copies, 1):
+            copy.wait_recv()
+            e, b, e_edge = received(d)
+            left += left_w[d] * e
+            right += right_w[d] * b - edge_w[d] * e_edge
+        for copy in copies:
+            copy.wait_send()
         return left, right
 
-    def line_scale(which):
-        a = jnp.exp(log_alpha(which))
-        return jnp.sqrt((1.0 - a) / (1.0 + a))
+    def tables(which):
+        size, at = ((nx, lane), (ny, sub))[which]
+        log_a = log_alpha(which)
+        a = jnp.exp(log_a)
+        scale = jnp.sqrt((1.0 - a) / (1.0 + a))
+        at = at.astype(f32)
+        own_ref[which] = scale.reshape(I * ny, nx)
+        near_ref[which] = (scale * jnp.exp(log_a * (at + 1.0))).reshape(I * ny, nx)
+        far_ref[which] = (scale * jnp.exp(log_a * (float(size) - at))).reshape(I * ny, nx)
 
     def east_copies(inst):
         return [
@@ -128,28 +183,20 @@
         return east_copies(inst)
 
     def east_finish(inst, copies):
-        for copy in copies:
-            copy.wait()
-        log_small = jnp.zeros((ny, nx), f32)
-        for i in range(I):
-            hit = (small_lane == i) | (small_lane == I + i)
-            log_small = jnp.where(hit, tab_ref[0, i * ny : (i + 1) * ny, :], log_small)
         left, right = combine(
-            None, None, log_small, col, C, nx,
+            east_table,
             (es_ref[inst, 0], es_ref[inst, 0], es_ref[inst, 1]),
             lambda d: (er_ref[inst, d, 0], er_ref[inst, d, 0], er_ref[inst, d, 1]),
-        )
-        at = lax.broadcasted_iota(jnp.int32, (ny, nx), 1).astype(f32)
+            copies,
+        )
         for i in range(I):
             rows = slice(i * ny, (i + 1) * ny)
-            log_a = tab_ref[0, rows, :]
             x = jnp.broadcast_to(left[:, i : i + 1], (ny, nx))
             y = jnp.broadcast_to(right[:, I + i : I + i + 1], (ny, nx))
-            a = jnp.exp(log_a)
-            lead_ref[rows, :] = jnp.sqrt((1.0 - a) / (1.0 + a)) * (
-                lead_ref[rows, :]
-                + jnp.exp(log_a * (at + 1.0)) * x
-                + jnp.exp(log_a * (float(nx) - at)) * y
+            lead_ref[rows, :] = (
+                own_ref[0, rows, :] * lead_ref[rows, :]
+                + near_ref[0, rows, :] * x
+                + far_ref[0, rows, :] * y
             )
 
     def north_start(u, inst):
@@ -162,34 +209,38 @@
         return north_copies(inst)
 
     def north_finish(inst, copies):
-        for copy in copies:
-            copy.wait()
-        log_small = tab_ref[1, pl.ds(0, I, stride=ny), :]
         left, right = combine(
-            None, None, log_small, row, R, ny,
+            north_table,
             (ns_ref[inst, 0], ns_ref[inst, 1], ns_ref[inst, 0]),
             lambda d: (nr_ref[inst, d, 0], nr_ref[inst, d, 1], nr_ref[inst, d, 0]),
-        )
-        at = lax.broadcasted_iota(jnp.int32, (ny, nx), 0).astype(f32)
+            copies,
+        )
         for i in range(I):
             rows = slice(i * ny, (i + 1) * ny)
-            log_a = tab_ref[1, rows, :]
             x = jnp.broadcast_to(left[i : i + 1, :], (ny, nx))
             y = jnp.broadcast_to(right[i : i + 1, :], (ny, nx))
-            a = jnp.exp(log_a)
-            lead_ref[rows, :] = jnp.sqrt((1.0 - a) / (1.0 + a)) * (
-                lead_ref[rows, :]
-                + jnp.exp(log_a * (at + 1.0)) * x
-                + jnp.exp(log_a * (float(ny) - at)) * y
+            lead_ref[rows, :] = (
+                own_ref[1, rows, :] * lead_ref[rows, :]
+                + near_ref[1, rows, :] * x
+                + far_ref[1, rows, :] * y
             )
 
-    plane = L * ny
     u = jnp.concatenate([dir_ref[v * plane : v * plane + M * ny, :] for v in range(V)], axis=0)
     copies = east_start(u.reshape(I, ny, nx), 0)
     pl.semaphore_wait(barrier, N - 1)
     for copy in copies:
         copy.start()
 
+    log_small = jnp.zeros((ny, nx), f32)
+    for i in range(I):
+        hit = (small_lane == i) | (small_lane == I + i)
+        log_small = jnp.where(hit, tab_ref[0, i * ny : (i + 1) * ny, :], log_small)
+    east_table = weights(log_small, col, C, nx)
+    tables(0)
+    for load in others:
+        load.wait()
+
+    pad = mix_ref.shape[1] // 2
     cell = cell_ref[...]
     slots = cell.shape[1]
     level = lax.shift_right_logical(cell, (ny * nx).bit_length() - 1)
@@ -198,38 +249,63 @@
         lax.broadcasted_iota(jnp.int32, (ny * nx, slots), 0) == spot, 1.0, 0.0
     ).astype(bf16)
     live = lax.broadcasted_iota(jnp.int32, (1, slots), 1) < cnt_ref[0]
-    weight = jnp.where(live, wgt_ref[...], 0.0)
-    parts = []
-    rest = weight
+    rest = jnp.where(live, wgt_ref[...], 0.0)
+    at = lax.broadcasted_iota(jnp.int32, (pad, slots), 0)
+    hits = [(at + v * L == level) & (at < L) for v in range(V)]
+    lhs = []
     for _ in range(3):
         part = rest.astype(bf16).astype(f32)
-        parts.append(part)
+        lhs += [jnp.where(hit, part, 0.0).astype(bf16) for hit in hits]
         rest = rest - part
-    nt = (((1,), (1,)), ((), ()))
-    for v in range(V):
-        hit = lax.broadcasted_iota(jnp.int32, (L, slots), 0) + v * L == level
+    summed = lax.dot_general(
+        jnp.concatenate(lhs, axis=0), hot_ref[...], (((1,), (1,)), ((), ())),
+        preferred_element_type=f32,
+    )
+    for v in range(V):
         wsum_ref[v] = sum(
-            lax.dot_general(
-                jnp.where(hit, part, 0.0).astype(bf16), hot_ref[...], nt,
-                preferred_element_type=f32,
-            )
-            for part in parts
-        )
+            summed[(n * V + v) * pad : (n * V + v + 1) * pad] for n in range(3)
+        )
+    mix_ref[...] = jnp.zeros_like(mix_ref)
+    for v in range(V):
+        mix_ref[v, 0:L, 0:L] = vm_ref[:, v, :] * amp_ref[v : v + 1, :]
 
     east_finish(0, copies)
     copies = north_start(lead_ref[...].reshape(I, ny, nx), 0)
     for copy in copies:
         copy.start()
+    north_table = weights(tab_ref[1, pl.ds(0, I, stride=ny), :], row, R, ny)
+    tables(1)
+
+    def split(x):
+        high = x.astype(bf16)
+        return high, (x - high.astype(f32)).astype(bf16)
+
+    def wide(x):
+        high = x.astype(bf16).astype(f32)
+        low = x - high
+        return jnp.concatenate(
+            [high + pltpu.roll(low, pad, 1), high], axis=1
+        )[0:pad, :].astype(bf16)
+
+    def tall(x):
+        high, low = split(x)
+        return jnp.concatenate([high, high, low, jnp.zeros_like(low)], axis=0)
+
+    sides = []
+    for v in range(V):
+        mixed = mix_ref[v]
+        sides.append((wide(mixed), wide(mixed.T)))
     north_finish(0, copies)
 
-    for v in range(V):
-        mixed = vm_ref[v] * amp_ref[v : v + 1, :]
+    spare = jnp.zeros((pad - L, nx), f32)
+    for v in range(V):
         field = jnp.concatenate(
             [
                 jnp.concatenate(
                     [
-                        lead_ref[pl.ds(v * M * ny + y, M, stride=ny), :],
-                        dir_ref[pl.ds(v * plane + M * ny + y, L - M, stride=ny), :],
+                        lead_ref[pl.ds(v * lead_rows + y, M, stride=ny), :],
+                        dir_ref[pl.ds(v * plane + lead_rows + y, L - M, stride=ny), :],
+                        spare,
                     ],
                     axis=0,
                 )
@@ -237,17 +313,10 @@
             ],
             axis=1,
         )
-        grid = lax.dot_general(
-            mixed, field, (((1,), (0,)), ((), ())),
-            precision=lax.Precision.HIGHEST, preferred_element_type=f32,
-        )
-        spread = grid * wsum_ref[v]
-        back = lax.dot_general(
-            mixed.T, spread, (((1,), (0,)), ((), ())),
-            precision=lax.Precision.HIGHEST, preferred_element_type=f32,
-        )
+        grid = jnp.dot(sides[v][0], tall(field), preferred_element_type=f32)
+        back = jnp.dot(sides[v][1], tall(grid * wsum_ref[v]), preferred_element_type=f32)
         for y in range(ny):
-            img_ref[pl.ds(v * plane + y, L, stride=ny), :] = back[:, y * nx : (y + 1) * nx]
+            img_ref[pl.ds(v * plane + y, L, stride=ny), :] = back[0:L, y * nx : (y + 1) * nx]
 
     u = jnp.concatenate([img_ref[v * plane : v * plane + M * ny, :] for v in range(V)], axis=0)
     copies = north_start(u.reshape(I, ny, nx), 1)
@@ -353,13 +422,6 @@
     norm_part = lax.fori_loop(0, steps, update, zero)
     rs_ref[1] = jnp.broadcast_to(jnp.sum(norm_part, axis=(0, 1), keepdims=True), (8, nx))
     reduce_start(1)
-    stores = [
-        pltpu.make_async_copy(oinc_ref, oinc_hbm, out_sem.at[0]),
-        pltpu.make_async_copy(ores_ref, ores_hbm, out_sem.at[1]),
-        pltpu.make_async_copy(odir_ref, odir_hbm, out_sem.at[2]),
-    ]
-    stores[0].start()
-    stores[1].start()
     ratio = jnp.broadcast_to(reduce_finish(1)[0:1, 0:1] / norm_old, (CHUNK, nx))
 
     def turn(s, carry):
@@ -368,9 +430,6 @@
         return carry
 
     lax.fori_loop(0, steps, turn, 0)
-    stores[2].start()
-    for store in stores:
-        store.wait()
 
 
 def local(
@@ -385,39 +444,44 @@
     N = R * C
     flat = V * L * ny
     slots = observed_cell.shape[0]
-    logs = jnp.stack([-1.0 / (length_east * nx), -1.0 / (length_north * ny)])
-    table = jnp.broadcast_to(logs.reshape(2, I, 1, 1), (2, I, ny, nx)).reshape(2, I * ny, nx)
-    vmem = pl.BlockSpec(memory_space=pltpu.VMEM)
-    hbm = pl.BlockSpec(memory_space=pl.ANY)
+    pad = (L + 15) // 16 * 16
+    hbm = pl.BlockSpec(memory_space=pltpu.HBM)
     smem = pl.BlockSpec(memory_space=pltpu.SMEM)
-    field = jax.ShapeDtypeStruct((flat, nx), f32)
+    field = pltpu.VMEM((V, L, ny, nx), f32)
+    near = pl.BlockSpec(memory_space=pltpu.VMEM)
     big = pltpu.VMEM((flat, nx), f32)
     out = pl.pallas_call(
         functools.partial(kernel, R, C, V, L, M, K, ny, nx, float(flat * nx * N)),
         out_shape=(field,) * 3,
-        in_specs=[vmem] * 6 + [smem] + [hbm] * 3,
-        out_specs=(hbm,) * 3,
+        in_specs=[smem] + [hbm] * 10,
+        out_specs=(near,) * 3,
         scratch_shapes=[
-            big, big, pltpu.VMEM((K, flat, nx), bf16), big, big, big,
+            big, pltpu.VMEM((2, V, M), f32), pltpu.VMEM((L, V, L), f32),
+            pltpu.VMEM((V, L), f32), pltpu.VMEM((1, slots), jnp.int32), pltpu.VMEM((1, slots), f32),
+            pltpu.VMEM((2, I * ny, nx), f32), pltpu.VMEM((2, I * ny, nx), f32),
+            pltpu.VMEM((2, I * ny, nx), f32), pltpu.VMEM((2, I * ny, nx), f32),
+            pltpu.VMEM((V, 2 * pad, 2 * pad), f32),
+            big, big, pltpu.VMEM((K, flat, nx), bf16),
             big, pltpu.VMEM((I * ny, nx), f32), pltpu.VMEM((2, I * ny, nx), f32),
-            pltpu.VMEM((ny * nx, slots), bf16), pltpu.VMEM((V, L, ny * nx), f32),
+            pltpu.VMEM((ny * nx, slots), bf16), pltpu.VMEM((V, pad, ny * nx), f32),
             pltpu.VMEM((2, 2, ny, nx), f32), pltpu.VMEM((2, C, 2, ny, nx), f32),
             pltpu.VMEM((2, 2, I, nx), f32), pltpu.VMEM((2, R, 2, I, nx), f32),
             pltpu.VMEM((2, 8, nx), f32), pltpu.VMEM((2, N, 8, nx), f32),
-            pltpu.SemaphoreType.DMA((3,)), pltpu.SemaphoreType.DMA((3,)),
+            pltpu.SemaphoreType.DMA((9 + 2 * V,)),
             pltpu.SemaphoreType.DMA((2, C)), pltpu.SemaphoreType.DMA((2, C)),
             pltpu.SemaphoreType.DMA((2, R)), pltpu.SemaphoreType.DMA((2, R)),
             pltpu.SemaphoreType.DMA((2, N)), pltpu.SemaphoreType.DMA((2, N)),
         ],
         compiler_params=pltpu.CompilerParams(
-            collective_id=0, has_side_effects=True, vmem_limit_bytes=48 * 2**20
+            collective_id=0, has_side_effects=True, vmem_limit_bytes=60 * 2**20
         ),
     )(
-        direction.reshape(flat, nx), table, vertical_modes, amplitude,
-        observed_cell.reshape(1, slots), observed_weight.reshape(1, slots), observed_count,
+        observed_count, direction.reshape(flat, nx), length_east, length_north,
+        jnp.transpose(vertical_modes, (1, 0, 2)), amplitude,
+        observed_cell.reshape(1, slots), observed_weight.reshape(1, slots),
         residual.reshape(flat, nx), increment.reshape(flat, nx), lanczos.reshape(K, flat, nx),
     )
-    return tuple(x.reshape(direction.shape) for x in out)
+    return tuple(out)
 
 
 def solution(mesh):

time: 53.9 us -> 45 us (0.83)
  local copies, waits for them, and re-layouts: 8.66 us -> 2.83 us
  Pallas kernels: 42.2 us -> 40.7 us
  other arithmetic: 1.39 us -> 0 us
    unnamed x14 -> x3, local copies, waits for them, and re-layouts: 8.19 us -> 2.83 us
    pallas_call x1, Pallas kernels: 42.2 us -> 40.7 us  [local(): pl.pallas_call(functools.partial(kernel, R, C, V, L, M, K, ny, nx, float(...]
    div x2 -> x0, other arithmetic: 1.38 us -> none  [local(): logs = jnp.stack([-1.0 / (length_east * nx), -1.0 / (length_north * ny)])]
where the time goes in v1:
time: 45 us; the launch traced here: 44.9 us
  Pallas kernels  40.7 us (90%)
  local copies, waits for them, and re-layouts  2.83 us (6%)
  between operations  1.29 us (3%)
    pallas_call x1, Pallas kernels, local(): pl.pallas_call(functools.partial(kernel, R, C, V, L, M, K, ny, nx, float(...  40.7 us
    unnamed x3, local copies, waits for them, and re-layouts  2.83 us

profile of v1, /device:TPU:0, one launch (start us, length us, event | category | flops | bytes accessed | tf_op | source)
XLA Modules:
  0.0 44.9 jit_solution(502966166307348564)
XLA Ops:
  1.3 40.7 %shard_map.130 = (f32[4,60,8,128]{3,2,1,0:T(8,128)S(1)}, f32[4,60,8,128]{3,2,1,0:T(8,128)S(1)}, f32[4,60,8,128]{3,2,1,0:T(8,128)S(1)}) custom-call(s32[1]{0:T(128)S(6)} %copy.20.cnt_ref, f32[1920,128]{1,0:T(8,128)} %bitcast.8, f32[4,8]{1,0:T(4,128)} %len_e_hbm.1, f32[4,8]{1,0:T(4,128)} %len_n_hbm.1, f32[60,4,60]{2,1,0:T(4,128)} %bitcast.11, ...), custom_call_target="tpu_custom_call" | custom-call | tf_op jit(solution)/shard_map/pallas_call | solution.py:453
  42.0 0.9 %copy.17 = f32[4,60,8,128]{3,2,1,0:T(8,128)} copy(f32[4,60,8,128]{3,2,1,0:T(8,128)S(1)} %get-tuple-element.3) | data formatting | bytes 1966080
  43.0 0.9 %copy.18 = f32[4,60,8,128]{3,2,1,0:T(8,128)} copy(f32[4,60,8,128]{3,2,1,0:T(8,128)S(1)} %get-tuple-element.4) | data formatting | bytes 1966080
  43.9 0.9 %copy.19 = f32[4,60,8,128]{3,2,1,0:T(8,128)} copy(f32[4,60,8,128]{3,2,1,0:T(8,128)S(1)} %get-tuple-element.5) | data formatting | bytes 1966080

commit v2 on v1

--- a/solution.py
+++ b/solution.py
@@ -362,29 +362,37 @@
 
     img_dots = lax.fori_loop(0, steps, second_dots, (zero,) * (K + 1))
 
-    def reduce_copy(inst, d):
+    def reduce_copy(inst, over, along):
         return pltpu.make_async_remote_copy(
             src_ref=rs_ref.at[inst],
-            dst_ref=rr_ref.at[inst, d],
-            send_sem=r_ssem.at[inst, d],
-            recv_sem=r_rsem.at[inst, d],
-            device_id=place(d),
+            dst_ref=rr_ref.at[inst, over * C + along],
+            send_sem=r_ssem.at[inst],
+            recv_sem=r_rsem.at[inst],
+            device_id=(lax.rem(row + over, R), lax.rem(col + along, C)),
             device_id_type=MESH,
         )
 
     def reduce_start(inst):
-        def go(d, carry):
-            reduce_copy(inst, d).start()
+        def go(over, carry):
+            for along in range(C):
+                reduce_copy(inst, over, along).start()
             return carry
 
-        lax.fori_loop(1, N, go, 0)
+        lax.fori_loop(1, R, go, 0)
+        for along in range(1, C):
+            reduce_copy(inst, 0, along).start()
 
     def reduce_finish(inst):
-        def go(d, carry):
-            reduce_copy(inst, d).wait()
-            return carry
-
-        lax.fori_loop(1, N, go, 0)
+        every = pltpu.make_async_remote_copy(
+            src_ref=rr_ref.at[inst, pl.ds(1, N - 1)],
+            dst_ref=rr_ref.at[inst, pl.ds(1, N - 1)],
+            send_sem=r_ssem.at[inst],
+            recv_sem=r_rsem.at[inst],
+            device_id=(row, lax.rem(col + 1, C)),
+            device_id_type=MESH,
+        )
+        every.wait_recv()
+        every.wait_send()
         rr_ref[inst, 0] = rs_ref[inst]
         return jnp.sum(rr_ref[inst], axis=0)
 
@@ -412,7 +420,6 @@
 
     def update(s, carry):
         rows = pl.ds(pl.multiple_of(s * CHUNK, CHUNK), CHUNK)
-        oinc_ref[rows, :] = inc_ref[rows, :] + step_wide * dir_ref[rows, :]
         moved = res_ref[rows, :] - step_wide * img_ref[rows, :]
         for k in range(K):
             moved = moved - coefficient[k] * lz_ref[k, rows, :].astype(f32)
@@ -422,6 +429,13 @@
     norm_part = lax.fori_loop(0, steps, update, zero)
     rs_ref[1] = jnp.broadcast_to(jnp.sum(norm_part, axis=(0, 1), keepdims=True), (8, nx))
     reduce_start(1)
+
+    def advance(s, carry):
+        rows = pl.ds(pl.multiple_of(s * CHUNK, CHUNK), CHUNK)
+        oinc_ref[rows, :] = inc_ref[rows, :] + step_wide * dir_ref[rows, :]
+        return carry
+
+    lax.fori_loop(0, steps, advance, 0, unroll=4)
     ratio = jnp.broadcast_to(reduce_finish(1)[0:1, 0:1] / norm_old, (CHUNK, nx))
 
     def turn(s, carry):
@@ -429,7 +443,7 @@
         odir_ref[rows, :] = ores_ref[rows, :] + ratio * dir_ref[rows, :]
         return carry
 
-    lax.fori_loop(0, steps, turn, 0)
+    lax.fori_loop(0, steps, turn, 0, unroll=4)
 
 
 def local(
@@ -470,7 +484,7 @@
             pltpu.SemaphoreType.DMA((9 + 2 * V,)),
             pltpu.SemaphoreType.DMA((2, C)), pltpu.SemaphoreType.DMA((2, C)),
             pltpu.SemaphoreType.DMA((2, R)), pltpu.SemaphoreType.DMA((2, R)),
-            pltpu.SemaphoreType.DMA((2, N)), pltpu.SemaphoreType.DMA((2, N)),
+            pltpu.SemaphoreType.DMA((2,)), pltpu.SemaphoreType.DMA((2,)),
         ],
         compiler_params=pltpu.CompilerParams(
             collective_id=0, has_side_effects=True, vmem_limit_bytes=60 * 2**20

time: 45 us -> 43.2 us (0.960)
  Pallas kernels: 40.7 us -> 38.9 us
    pallas_call x1, Pallas kernels: 40.7 us -> 38.9 us  [local(): pl.pallas_call(functools.partial(kernel, R, C, V, L, M, K, ny, nx, float(...]
where the time goes in v2:
time: 43.2 us; the launch traced here: 43 us
  Pallas kernels  38.9 us (90%)
  local copies, waits for them, and re-layouts  2.83 us (7%)
  between operations  1.29 us (3%)
    pallas_call x1, Pallas kernels, local(): pl.pallas_call(functools.partial(kernel, R, C, V, L, M, K, ny, nx, float(...  38.9 us
    unnamed x3, local copies, waits for them, and re-layouts  2.83 us

profile of v2, /device:TPU:0, one launch (start us, length us, event | category | flops | bytes accessed | tf_op | source)
XLA Modules:
  0.0 43.0 jit_solution(7273090499278856706)
XLA Ops:
  1.3 38.9 %shard_map.130 = (f32[4,60,8,128]{3,2,1,0:T(8,128)S(1)}, f32[4,60,8,128]{3,2,1,0:T(8,128)S(1)}, f32[4,60,8,128]{3,2,1,0:T(8,128)S(1)}) custom-call(s32[1]{0:T(128)S(6)} %copy.20.cnt_ref, f32[1920,128]{1,0:T(8,128)} %bitcast.8, f32[4,8]{1,0:T(4,128)} %len_e_hbm.1, f32[4,8]{1,0:T(4,128)} %len_n_hbm.1, f32[60,4,60]{2,1,0:T(4,128)} %bitcast.11, ...), custom_call_target="tpu_custom_call" | custom-call | tf_op jit(solution)/shard_map/pallas_call | solution.py:467
  40.2 0.9 %copy.17 = f32[4,60,8,128]{3,2,1,0:T(8,128)} copy(f32[4,60,8,128]{3,2,1,0:T(8,128)S(1)} %get-tuple-element.3) | data formatting | bytes 1966080
  41.1 0.9 %copy.18 = f32[4,60,8,128]{3,2,1,0:T(8,128)} copy(f32[4,60,8,128]{3,2,1,0:T(8,128)S(1)} %get-tuple-element.4) | data formatting | bytes 1966080
  42.0 0.9 %copy.19 = f32[4,60,8,128]{3,2,1,0:T(8,128)} copy(f32[4,60,8,128]{3,2,1,0:T(8,128)S(1)} %get-tuple-element.5) | data formatting | bytes 1966080

commit v3 on v2

--- a/solution.py
+++ b/solution.py
@@ -360,7 +360,7 @@
             out.append(carry[k + 1] + fold(image * lz_ref[k, rows, :].astype(f32)))
         return tuple(out)
 
-    img_dots = lax.fori_loop(0, steps, second_dots, (zero,) * (K + 1))
+    img_dots = lax.fori_loop(0, steps, second_dots, (zero,) * (K + 1), unroll=2)
 
     def reduce_copy(inst, over, along):
         return pltpu.make_async_remote_copy(
@@ -426,7 +426,7 @@
         ores_ref[rows, :] = moved
         return carry + fold(moved * moved)
 
-    norm_part = lax.fori_loop(0, steps, update, zero)
+    norm_part = lax.fori_loop(0, steps, update, zero, unroll=2)
     rs_ref[1] = jnp.broadcast_to(jnp.sum(norm_part, axis=(0, 1), keepdims=True), (8, nx))
     reduce_start(1)
 

time: 43.2 us -> 42.7 us (0.988)
  Pallas kernels: 38.9 us -> 38.4 us
    pallas_call x1, Pallas kernels: 38.9 us -> 38.4 us  [local(): pl.pallas_call(functools.partial(kernel, R, C, V, L, M, K, ny, nx, float(...]
where the time goes in v3:
time: 42.7 us; the launch traced here: 42.5 us
  Pallas kernels  38.4 us (90%)
  local copies, waits for them, and re-layouts  2.83 us (7%)
  between operations  1.29 us (3%)
    pallas_call x1, Pallas kernels, local(): pl.pallas_call(functools.partial(kernel, R, C, V, L, M, K, ny, nx, float(...  38.4 us
    unnamed x3, local copies, waits for them, and re-layouts  2.83 us

profile of v3, /device:TPU:0, one launch (start us, length us, event | category | flops | bytes accessed | tf_op | source)
XLA Modules:
  0.0 42.5 jit_solution(1356597148665520543)
XLA Ops:
  1.3 38.4 %shard_map.130 = (f32[4,60,8,128]{3,2,1,0:T(8,128)S(1)}, f32[4,60,8,128]{3,2,1,0:T(8,128)S(1)}, f32[4,60,8,128]{3,2,1,0:T(8,128)S(1)}) custom-call(s32[1]{0:T(128)S(6)} %copy.20.cnt_ref, f32[1920,128]{1,0:T(8,128)} %bitcast.8, f32[4,8]{1,0:T(4,128)} %len_e_hbm.1, f32[4,8]{1,0:T(4,128)} %len_n_hbm.1, f32[60,4,60]{2,1,0:T(4,128)} %bitcast.11, ...), custom_call_target="tpu_custom_call" | custom-call | tf_op jit(solution)/shard_map/pallas_call | solution.py:467
  39.7 0.9 %copy.17 = f32[4,60,8,128]{3,2,1,0:T(8,128)} copy(f32[4,60,8,128]{3,2,1,0:T(8,128)S(1)} %get-tuple-element.3) | data formatting | bytes 1966080
  40.6 0.9 %copy.18 = f32[4,60,8,128]{3,2,1,0:T(8,128)} copy(f32[4,60,8,128]{3,2,1,0:T(8,128)S(1)} %get-tuple-element.4) | data formatting | bytes 1966080
  41.5 0.9 %copy.19 = f32[4,60,8,128]{3,2,1,0:T(8,128)} copy(f32[4,60,8,128]{3,2,1,0:T(8,128)S(1)} %get-tuple-element.5) | data formatting | bytes 1966080
